TPU v7x, 32 devices: a whole 2x2x4 slice. The times are simulated.
32 devices in a mesh: row: 8 (over y, x, core), col: 4 (over z).
Axes of the slice: x: 2, y: 2, z: 4, core: 2. Of those that a mesh axis runs over, the one named last changes fastest.
Arguments:
- matrix: float32 [5120, 5120], P('row', 'col'), may hold values from -64 to 64
Outputs:
- iterate: float32 [5120, 5120], P('row', 'col')
- trace_value: float32 [2], replicated
- frobenius: float32 [2], replicated
All inputs are finite; a program needn't handle non-finite values.
Results may differ from a plain program's by a relative error of at most 0.003.
Values may be sent and summed in bfloat16 or wider, within the bound.
A program may use at most 64 MiB of HBM per device.

v0:
```python
import jax
import jax.numpy as jnp
from jax import lax
from jax.sharding import PartitionSpec as P

ITERS = 2


target = 0.0625


def add_columns(portion, left_panel):
    return jnp.dot(left_panel, portion, preferred_element_type=jnp.float32)


def on_device(matrix):
    rounded = matrix.astype(jnp.bfloat16)
    current = rounded.astype(jnp.float32)
    row_ids = lax.axis_index("row") * matrix.shape[0] + lax.broadcasted_iota(
        jnp.int32, matrix.shape, 0
    )
    col_ids = lax.axis_index("col") * matrix.shape[1] + lax.broadcasted_iota(
        jnp.int32, matrix.shape, 1
    )
    on_diagonal = row_ids == col_ids
    traces = []
    norms = []
    for step in range(ITERS):
        row_panel = lax.all_gather(rounded, "col", axis=1, tiled=True)
        if step == 0:
            order_full = row_panel.shape[1]
            squares = lax.psum(jnp.sum(current * current), ("row", "col"))
            scale = target * order_full / (squares + 1e-06)
            root = jnp.sqrt(scale)
        else:
            scale = jnp.float32(1.0)
            root = jnp.float32(1.0)
        product = add_columns(
            lax.all_gather(rounded, "row", axis=0, tiled=True), left_panel=row_panel
        )
        squared = (product * scale).astype(jnp.bfloat16)
        cubic_part = add_columns(
            lax.all_gather(squared, "row", axis=0, tiled=True), left_panel=row_panel
        )
        current = root * (1.5 * current - 0.5 * cubic_part)
        rounded = current.astype(jnp.bfloat16)
        diagonal_part = jnp.sum(jnp.where(on_diagonal, current, 0.0))
        square_part = jnp.sum(current * current)
        trace_now, total_now = lax.psum((diagonal_part, square_part), ("row", "col"))
        traces.append(trace_now)
        norms.append(jnp.sqrt(total_now))
    return (current, jnp.stack(traces), jnp.stack(norms))


def solution(mesh):
    in_specs = (P("row", "col"),)
    out_specs = (P("row", "col"), P(), P())
    return jax.shard_map(
        on_device, mesh=mesh, in_specs=in_specs, out_specs=out_specs, check_vma=False
    )
```

profile of v0, /device:TPU:0, one launch (start us, length us, event | category | flops | bytes accessed | tf_op | source)
XLA Modules:
  0.0 667.8 jit_solution(10903226945213668132)
XLA Ops:
  7.2 4.0 copy.4
  11.2 0.0 all-gather.9.cloned.1.call-start
  11.3 0.7 all-gather.9.cloned.1.call-update
  12.0 0.0 all-gather.11.cloned.1.call-start
  12.0 0.6 copy-done
  12.6 1.4 fusion.4
  14.1 51.2 %psum.35 = f32[]{:T(128)} all-reduce(f32[]{:T(128)} %fusion.4), channel_id=1, replica_groups=mesh['row'=8,'col'=4] {'row','col'}, use_global_device_ids=true, to_apply=%region_1.0 | all-reduce | flops 1 | bytes 8 | tf_op jit(solution)/shard_map/psum | solution.py:32
  65.9 68.8 %all-gather.7.cloned.1.call-done = bf16[640,5120]{0,1:T(8,128)(2,1)} async-done(((bf16[640,1280]{0,1:T(8,128)(2,1)}), bf16[640,5120]{0,1:T(8,128)(2,1)}) %all-gather.7.cloned.1.call-update) | async-done | bytes 6553616 | tf_op jit(solution)/shard_map/all_gather | solution.py:29
  134.8 74.7 %all-gather.9.cloned.1.call-done = bf16[5120,1280]{0,1:T(8,128)(2,1)} async-done(((bf16[640,1280]{0,1:T(8,128)(2,1)}), bf16[5120,1280]{0,1:T(8,128)(2,1)}) %all-gather.9.cloned.1.call-update) | async-done | bytes 13107216 | tf_op jit(solution)/shard_map/all_gather | solution.py:39
  209.4 14.1 %fusion.7 = bf16[640,1280]{1,0:T(8,128)(2,1)} fusion(bf16[640,5120]{0,1:T(8,128)(2,1)} %all-gather.7.cloned.1.call-done, bf16[5120,1280]{0,1:T(8,128)(2,1)} %all-gather.9.cloned.1.call-done, f32[]{:T(128)S(6)} %div.3), kind=kOutput, calls=%fused_computation.16 | convolution fusion | flops 8390246400 | bytes 21299204 | tf_op jit(solution)/shard_map/dot_general | solution.py:13
  223.6 0.0 all-gather.13.cloned.1.call-start
  223.7 74.2 %all-gather.11.cloned.1.call-done = bf16[5120,1280]{1,0:T(8,128)(2,1)} async-done(((bf16[640,1280]{1,0:T(8,128)(2,1)}), bf16[5120,1280]{1,0:T(8,128)(2,1)}) %all-gather.11.cloned.1.call-update) | async-done | bytes 13107216 | tf_op jit(solution)/shard_map/all_gather | solution.py:43
  297.9 18.0 %multiply_reduce_fusion.1 = (f32[]{:T(128)}, f32[]{:T(128)}, bf16[640,1280]{0,1:T(8,128)(2,1)}, f32[640,1280]{0,1:T(8,128)}) fusion(s32[1280]{0:T(1024)S(1)} %iota_add_fusion, s32[640]{0:T(1024)S(1)} %iota_add_fusion.1, bf16[5120,1280]{1,0:T(8,128)(2,1)} %all-gather.11.cloned.1.call-done, bf16[640,5120]{0,1:T(8,128)(2,1)} %all-gather.7.cloned.1.call-done, ...), kind=kOutput, calls=%fused_computation.15 | convolution fusion | flops 8397619200 | bytes 26222092 | tf_op jit(solution)/shard_map/dot_general | solution.py:13
  316.0 0.0 all-gather.15.cloned.1.call-start
  316.0 0.5 all-gather.15.cloned.1.call-update
  316.6 0.2 all-gather.17.cloned.1.call-start
  316.8 118.9 %all-gather.13.cloned.1.call-done = bf16[640,5120]{0,1:T(8,128)(2,1)} async-done(((bf16[640,1280]{0,1:T(8,128)(2,1)}), bf16[640,5120]{0,1:T(8,128)(2,1)}) %all-gather.13.cloned.1.call-update) | async-done | bytes 6553616 | tf_op jit(solution)/shard_map/all_gather | solution.py:29
  435.7 74.0 %all-gather.15.cloned.1.call-done = bf16[5120,1280]{0,1:T(8,128)(2,1)} async-done(((bf16[640,1280]{0,1:T(8,128)(2,1)}), bf16[5120,1280]{0,1:T(8,128)(2,1)}) %all-gather.15.cloned.1.call-update) | async-done | bytes 13107216 | tf_op jit(solution)/shard_map/all_gather | solution.py:39
  509.7 14.1 %convolution_convert_fusion = bf16[640,1280]{1,0:T(8,128)(2,1)} fusion(bf16[640,5120]{0,1:T(8,128)(2,1)} %all-gather.13.cloned.1.call-done, bf16[5120,1280]{0,1:T(8,128)(2,1)} %all-gather.15.cloned.1.call-done), kind=kOutput, calls=%fused_computation.17 | convolution fusion | flops 8389427200 | bytes 21299200 | tf_op jit(solution)/shard_map/dot_general | solution.py:13
  523.8 74.4 %all-gather.17.cloned.1.call-done = bf16[5120,1280]{1,0:T(8,128)(2,1)} async-done(((bf16[640,1280]{1,0:T(8,128)(2,1)}), bf16[5120,1280]{1,0:T(8,128)(2,1)}) %all-gather.17.cloned.1.call-update) | async-done | bytes 13107216 | tf_op jit(solution)/shard_map/all_gather | solution.py:43
  598.2 17.0 %multiply_reduce_fusion = (f32[]{:T(128)}, f32[]{:T(128)}, f32[640,1280]{0,1:T(8,128)S(1)}) fusion(s32[1280]{0:T(1024)S(1)} %iota_add_fusion, s32[640]{0:T(1024)S(1)} %iota_add_fusion.1, bf16[640,5120]{0,1:T(8,128)(2,1)} %all-gather.13.cloned.1.call-done, bf16[5120,1280]{1,0:T(8,128)(2,1)} %all-gather.17.cloned.1.call-done, f32[640,1280]{0,1:T(8,128)} %get-tuple-element.15), kind=kOutput, calls=%fused_computation.14 | convolution fusion | flops 8395161600 | bytes 26222088 | tf_op jit(solution)/shard_map/dot_general | solution.py:13
  615.2 2.9 copy.6
  618.1 39.6 %all-reduce = (f32[1]{0:T(128)}, f32[1]{0:T(128)}, f32[]{:T(128)}, f32[]{:T(128)}) all-reduce(f32[1]{0:T(128)} %bitcast.2, f32[1]{0:T(128)} %bitcast.1, f32[]{:T(128)} %get-tuple-element.8, f32[]{:T(128)} %get-tuple-element.6), channel_id=1, replica_groups=mesh['row'=8,'col'=4] {'row','col'}, use_global_device_ids=true, to_apply=%region_5.6 | all-reduce | flops 4 | bytes 32 | tf_op jit(solution)/shard_map/psum | solution.py:49
  659.1 1.8 pad_maximum_fusion
  (8 shorter events, 0.1 us)
Async XLA Ops:
  7.2 127.6 %all-gather.7.cloned.1.call-start = ((), (), s32[]{:S(2)}) async-start(), calls=%async_computation | async-start | bytes 8192000 | tf_op jit(solution)/shard_map/all_gather | solution.py:29
  11.2 1.4 copy-start
  11.2 198.2 %all-gather.9.cloned.1.call-start = ((), (), s32[]{:S(2)}) async-start(), calls=%async_computation.1 | async-start | bytes 14745600 | tf_op jit(solution)/shard_map/all_gather | solution.py:39
  12.0 286.0 %all-gather.11.cloned.1.call-start = ((), (), s32[]{:S(2)}) async-start(), calls=%async_computation.2 | async-start | bytes 14745600 | tf_op jit(solution)/shard_map/all_gather | solution.py:43
  223.6 212.2 %all-gather.13.cloned.1.call-start = ((), (), s32[]{:S(2)}) async-start(), calls=%async_computation.3 | async-start | bytes 8192000 | tf_op jit(solution)/shard_map/all_gather | solution.py:29
  316.0 193.8 %all-gather.15.cloned.1.call-start = ((), (), s32[]{:S(2)}) async-start(), calls=%async_computation.4 | async-start | bytes 14745600 | tf_op jit(solution)/shard_map/all_gather | solution.py:39
  316.6 281.6 %all-gather.17.cloned.1.call-start = ((), (), s32[]{:S(2)}) async-start(), calls=%async_computation.5 | async-start | bytes 14745600 | tf_op jit(solution)/shard_map/all_gather | solution.py:43
Sparse Core Ops, SparseCore 0:
  11.3 123.3 all-gather.6
  137.2 72.1 all-gather.8
  223.7 74.1 all-gather.10
  316.1 119.5 all-gather.12
  437.5 72.2 all-gather.14
  524.0 74.1 all-gather.16
where the time goes:
time: 668 us
  waiting for transfers between devices  486 us (73%)
  blocking collectives  90.8 us (14%)
  matrix products  63.2 us (9%)
  between operations  16.2 us (2%)
  local copies, waits for them, and re-layouts  7.52 us (1%)
    all_gather x2, waiting for transfers between devices, on_device(): row_panel = lax.all_gather(rounded, 'col', axis=1, tiled=True)  188 us
    all_gather x2, waiting for transfers between devices, on_device(): lax.all_gather(rounded, 'row', axis=0, tiled=True)  149 us
    all_gather x2, waiting for transfers between devices, on_device(): lax.all_gather(squared, 'row', axis=0, tiled=True)  149 us
    dot_general x4, matrix products, add_columns(): return jnp.dot(left_panel, portion, preferred_element_type=jnp.float32)  63.2 us
    psum x1, blocking collectives, on_device(): squares = lax.psum(jnp.sum(current * current), ('row', 'col'))  51.2 us
    psum x1, blocking collectives, on_device(): lax.psum((diagonal_part, square_part), ('row', 'col'))  39.6 us
  transfers between devices with their start and end apart: 6, of which 6 were waited for; matrix products, arithmetic and copies ran while one was open for 0% of the time, Pallas kernels for 0%

commit v1 on v0

--- a/solution.py
+++ b/solution.py
@@ -1,10 +1,15 @@
+import functools
+
 import jax
 import jax.numpy as jnp
 from jax import lax
+from jax.experimental import pallas as pl
+from jax.experimental.pallas import tpu as pltpu
 from jax.sharding import PartitionSpec as P
 
 ITERS = 2
-
+TILE = 256
+MESH = pl.DeviceIdType.MESH
 
 target = 0.0625
 
@@ -52,9 +57,395 @@
     return (current, jnp.stack(traces), jnp.stack(norms))
 
 
+FROM_X, FROM_Y, FROM_SIB, SIB_X, SIB_Y, FROM_D, SIB_D = range(7)
+KINDS = 7
+
+
+def kernel(
+    n_row,
+    n_col,
+    matrix_ref,
+    out_ref,
+    trace_ref,
+    frob_ref,
+    panel1,
+    panel2,
+    cols,
+    squares,
+    current,
+    stats,
+    slots_row,
+    slots_col,
+    xy_send,
+    xy_recv,
+    z_send,
+    z_recv,
+    red_send,
+    red_recv,
+    load_sem,
+    store_sem,
+):
+    rows, width = matrix_ref.shape
+    tiles = width // TILE
+    half = rows // 2
+    order = rows * n_row
+    r = lax.axis_index("row")
+    z = lax.axis_index("col")
+    core = lax.rem(r, 2)
+    x = lax.rem(r // 2, 2)
+    y = r // 4
+    to_sib = 1 - 2 * core
+    rs = r + to_sib
+    rx = r + 2 - 4 * x
+    ry = r + 4 - 8 * y
+    rd = rx + 4 - 8 * y
+    relay_from = ry * (1 - core) + rx * core
+    relay_to = rx * (1 - core) + ry * core
+    up = lax.rem(z + 1, n_col)
+    down = lax.rem(z + n_col - 1, n_col)
+    opposite = lax.rem(z + 2, n_col)
+
+    def load(t):
+        return pltpu.make_async_copy(
+            matrix_ref.at[:, pl.ds(t * TILE, TILE)], current.at[t], load_sem.at[t]
+        )
+
+    def store(t):
+        return pltpu.make_async_copy(
+            current.at[t],
+            out_ref.at[:, pl.ds(pl.multiple_of(t * TILE, TILE), TILE)],
+            store_sem.at[t],
+        )
+
+    for t in range(tiles):
+        load(t).start()
+
+    barrier = pltpu.get_barrier_semaphore()
+    for j in range(1, n_row):
+        pl.semaphore_signal(
+            barrier, inc=1, device_id={"row": lax.rem(r + j, n_row)}, device_id_type=MESH
+        )
+    for j in range(1, n_col):
+        pl.semaphore_signal(
+            barrier, inc=1, device_id={"col": lax.rem(z + j, n_col)}, device_id_type=MESH
+        )
+    pl.semaphore_wait(barrier, n_row + n_col - 2)
+
+    def rows_of(slot):
+        return pl.ds(pl.multiple_of(slot * rows, rows), rows)
+
+    def columns_of(slot, t):
+        return pl.ds(pl.multiple_of(slot * width + t * TILE, TILE), TILE)
+
+    def xy(buf, phase, t, slot, kind, peer):
+        part = buf.at[t, rows_of(slot), :]
+        return pltpu.make_async_remote_copy(
+            src_ref=part,
+            dst_ref=part,
+            send_sem=xy_send.at[phase, t, kind],
+            recv_sem=xy_recv.at[phase, t, kind],
+            device_id={"row": peer},
+            device_id_type=MESH,
+        )
+
+    def xy_start(buf, phase, t):
+        xy(buf, phase, t, r, FROM_X, rx).start()
+        xy(buf, phase, t, r, FROM_Y, ry).start()
+        xy(buf, phase, t, r, FROM_SIB, rs).start()
+
+    def xy_mid(buf, phase, t):
+        xy(buf, phase, t, rx, FROM_X, rx).wait_recv()
+        xy(buf, phase, t, ry, FROM_Y, ry).wait_recv()
+        xy(buf, phase, t, relay_from, FROM_D, relay_to).start()
+        xy(buf, phase, t, rx, SIB_X, rs).start()
+        xy(buf, phase, t, ry, SIB_Y, rs).start()
+
+    def xy_fin(buf, phase, t):
+        xy(buf, phase, t, rd, FROM_D, rd).wait_recv()
+        xy(buf, phase, t, rd, SIB_D, rs).start()
+
+    def xy_done(buf, phase, t):
+        xy(buf, phase, t, rs, FROM_SIB, rs).wait_recv()
+        xy(buf, phase, t, rx + to_sib, SIB_X, rs).wait_recv()
+        xy(buf, phase, t, ry + to_sib, SIB_Y, rs).wait_recv()
+        xy(buf, phase, t, rd + to_sib, SIB_D, rs).wait_recv()
+
+    def xy_sent(buf, phase, t):
+        xy(buf, phase, t, r, FROM_X, rx).wait_send()
+        xy(buf, phase, t, r, FROM_Y, ry).wait_send()
+        xy(buf, phase, t, r, FROM_SIB, rs).wait_send()
+        xy(buf, phase, t, rx, SIB_X, rs).wait_send()
+        xy(buf, phase, t, ry, SIB_Y, rs).wait_send()
+        xy(buf, phase, t, relay_from, FROM_D, relay_to).wait_send()
+        xy(buf, phase, t, rd, SIB_D, rs).wait_send()
+
+    def zc(panel, step, t, slot, kind, peer):
+        if kind < 2:
+            part = panel.at[:, columns_of(slot, t)]
+        else:
+            part = panel.at[pl.ds((kind - 2) * half, half), columns_of(slot, t)]
+        return pltpu.make_async_remote_copy(
+            src_ref=part,
+            dst_ref=part,
+            send_sem=z_send.at[step, t, kind],
+            recv_sem=z_recv.at[step, t, kind],
+            device_id={"col": peer},
+            device_id_type=MESH,
+        )
+
+    def z_start(panel, step, t):
+        zc(panel, step, t, z, 0, up).start()
+        zc(panel, step, t, z, 1, down).start()
+
+    def z_mid(panel, step, t):
+        zc(panel, step, t, down, 0, up).wait_recv()
+        zc(panel, step, t, down, 2, up).start()
+        zc(panel, step, t, up, 1, down).wait_recv()
+        zc(panel, step, t, up, 3, down).start()
+
+    def z_fin(panel, step, t):
+        zc(panel, step, t, opposite, 2, up).wait_recv()
+        zc(panel, step, t, opposite, 3, down).wait_recv()
+
+    def z_sent(panel, step, t):
+        zc(panel, step, t, z, 0, up).wait_send()
+        zc(panel, step, t, z, 1, down).wait_send()
+        zc(panel, step, t, down, 2, up).wait_send()
+        zc(panel, step, t, up, 3, down).wait_send()
+
+    def red_row(which, j, slot, peer):
+        part = slots_row.at[which, slot]
+        return pltpu.make_async_remote_copy(
+            src_ref=part,
+            dst_ref=part,
+            send_sem=red_send.at[which, j],
+            recv_sem=red_recv.at[which, j],
+            device_id={"row": peer},
+            device_id_type=MESH,
+        )
+
+    def red_col(which, j, slot, peer):
+        part = slots_col.at[which, slot]
+        return pltpu.make_async_remote_copy(
+            src_ref=part,
+            dst_ref=part,
+            send_sem=red_send.at[which, n_row + j],
+            recv_sem=red_recv.at[which, n_row + j],
+            device_id={"col": peer},
+            device_id_type=MESH,
+        )
+
+    def reduce_start(which, value):
+        slots_row[which, r] = value
+        for j in range(1, n_row):
+            red_row(which, j, r, lax.rem(r + j, n_row)).start()
+
+    def reduce_mid(which):
+        for j in range(1, n_row):
+            back = lax.rem(r + n_row - j, n_row)
+            red_row(which, j, back, back).wait_recv()
+        total = slots_row[which, 0]
+        for s in range(1, n_row):
+            total = total + slots_row[which, s]
+        slots_col[which, z] = total
+        for j in range(1, n_col):
+            red_col(which, j, z, lax.rem(z + j, n_col)).start()
+
+    def reduce_end(which):
+        for j in range(1, n_col):
+            back = lax.rem(z + n_col - j, n_col)
+            red_col(which, j, back, back).wait_recv()
+        total = slots_col[which, 0]
+        for s in range(1, n_col):
+            total = total + slots_col[which, s]
+        for j in range(1, n_row):
+            red_row(which, j, r, lax.rem(r + j, n_row)).wait_send()
+        for j in range(1, n_col):
+            red_col(which, j, z, lax.rem(z + j, n_col)).wait_send()
+        return total
+
+    def lanes(v):
+        s = jnp.sum(v, axis=0, keepdims=True)
+        out = s[:, 0:128]
+        for i in range(1, TILE // 128):
+            out = out + s[:, i * 128 : (i + 1) * 128]
+        return out
+
+    def add_stats(k, t, v):
+        row_ids = r * rows + lax.broadcasted_iota(jnp.int32, v.shape, 0)
+        col_ids = z * width + t * TILE + lax.broadcasted_iota(jnp.int32, v.shape, 1)
+        stats[k : k + 1, :] += lanes(jnp.where(row_ids == col_ids, v, 0.0))
+        stats[k + 1 : k + 2, :] += lanes(v * v)
+
+    stats[...] = jnp.zeros_like(stats)
+    for t in range(tiles):
+        load(t).wait()
+        rounded = current[t].astype(jnp.bfloat16)
+        panel1[:, columns_of(z, t)] = rounded
+        cols[t, rows_of(r), :] = rounded
+        xy_start(cols, 0, t)
+        z_start(panel1, 0, t)
+        wide = rounded.astype(jnp.float32)
+        stats[4:5, :] += lanes(wide * wide)
+    reduce_start(0, stats[...])
+    reduce_mid(0)
+
+    def product_phase(step, panel, scale):
+        phase = 2 * step
+
+        def mid(t, carry):
+            xy_mid(cols, phase, t)
+            z_mid(panel, step, t)
+            return carry
+
+        lax.fori_loop(0, tiles, mid, 0)
+
+        def fin(t, carry):
+            z_fin(panel, step, t)
+            return carry
+
+        lax.fori_loop(0, tiles, fin, 0)
+        xy_fin(cols, phase, 0)
+
+        def work(t, carry):
+            @pl.when(t < tiles - 1)
+            def _():
+                xy_fin(cols, phase, t + 1)
+
+            xy_done(cols, phase, t)
+            product = jnp.dot(panel[...], cols[t], preferred_element_type=jnp.float32)
+            if scale is not None:
+                product = product * scale
+            squares[t, rows_of(r), :] = product.astype(jnp.bfloat16)
+            xy_sent(cols, phase, t)
+            xy_start(squares, phase + 1, t)
+            return carry
+
+        lax.fori_loop(0, tiles, work, 0)
+
+    def cubic_phase(step, panel, finish):
+        phase = 2 * step + 1
+
+        def mid(t, carry):
+            xy_mid(squares, phase, t)
+            return carry
+
+        lax.fori_loop(0, tiles, mid, 0)
+        xy_fin(squares, phase, 0)
+
+        def work(t, carry):
+            @pl.when(t < tiles - 1)
+            def _():
+                xy_fin(squares, phase, t + 1)
+
+            xy_done(squares, phase, t)
+            cubic = jnp.dot(panel[...], squares[t], preferred_element_type=jnp.float32)
+            xy_sent(squares, phase, t)
+            finish(t, cubic)
+            return carry
+
+        lax.fori_loop(0, tiles, work, 0)
+
+    total = reduce_end(0)
+    scale = target * order / (jnp.sum(total[4:5, :], axis=1, keepdims=True) + 1e-06)
+    root = jnp.sqrt(scale)
+
+    product_phase(0, panel1, scale)
+
+    def finish_first(t, cubic):
+        wide = panel1[:, columns_of(z, t)].astype(jnp.float32)
+        value = root * (1.5 * wide - 0.5 * cubic)
+        current[t] = value
+        rounded = value.astype(jnp.bfloat16)
+        panel2[:, columns_of(z, t)] = rounded
+        cols[t, rows_of(r), :] = rounded
+        xy_start(cols, 2, t)
+        z_start(panel2, 1, t)
+        add_stats(0, t, value)
+
+    cubic_phase(0, panel1, finish_first)
+    product_phase(1, panel2, None)
+
+    def finish_second(t, cubic):
+        value = 1.5 * current[t] - 0.5 * cubic
+        current[t] = value
+        store(t).start()
+        add_stats(2, t, value)
+
+    cubic_phase(1, panel2, finish_second)
+
+    reduce_start(1, stats[...])
+    reduce_mid(1)
+    total = reduce_end(1)
+    sums = jnp.sum(total, axis=1, keepdims=True)
+    norms = jnp.sqrt(sums)
+    trace_ref[0] = sums[0, 0]
+    trace_ref[1] = sums[2, 0]
+    frob_ref[0] = norms[1, 0]
+    frob_ref[1] = norms[3, 0]
+
+    def clear(t, carry):
+        z_sent(panel1, 0, t)
+        z_sent(panel2, 1, t)
+        store(t).wait()
+        return carry
+
+    lax.fori_loop(0, tiles, clear, 0)
+
+
+def in_one_kernel(n_row, n_col, matrix):
+    rows, width = matrix.shape
+    tiles = width // TILE
+    order = rows * n_row
+    narrow = jnp.bfloat16
+    return pl.pallas_call(
+        functools.partial(kernel, n_row, n_col),
+        out_shape=(
+            jax.ShapeDtypeStruct((rows, width), jnp.float32),
+            jax.ShapeDtypeStruct((ITERS,), jnp.float32),
+            jax.ShapeDtypeStruct((ITERS,), jnp.float32),
+        ),
+        in_specs=[pl.BlockSpec(memory_space=pl.ANY)],
+        out_specs=(
+            pl.BlockSpec(memory_space=pl.ANY),
+            pl.BlockSpec(memory_space=pltpu.SMEM),
+            pl.BlockSpec(memory_space=pltpu.SMEM),
+        ),
+        scratch_shapes=[
+            pltpu.VMEM((rows, width * n_col), narrow),
+            pltpu.VMEM((rows, width * n_col), narrow),
+            pltpu.VMEM((tiles, order, TILE), narrow),
+            pltpu.VMEM((tiles, order, TILE), narrow),
+            pltpu.VMEM((tiles, rows, TILE), jnp.float32),
+            pltpu.VMEM((8, 128), jnp.float32),
+            pltpu.VMEM((2, n_row, 8, 128), jnp.float32),
+            pltpu.VMEM((2, n_col, 8, 128), jnp.float32),
+            pltpu.SemaphoreType.DMA((2 * ITERS, tiles, KINDS)),
+            pltpu.SemaphoreType.DMA((2 * ITERS, tiles, KINDS)),
+            pltpu.SemaphoreType.DMA((ITERS, tiles, 4)),
+            pltpu.SemaphoreType.DMA((ITERS, tiles, 4)),
+            pltpu.SemaphoreType.DMA((2, n_row + n_col)),
+            pltpu.SemaphoreType.DMA((2, n_row + n_col)),
+            pltpu.SemaphoreType.DMA((tiles,)),
+            pltpu.SemaphoreType.DMA((tiles,)),
+        ],
+        compiler_params=pltpu.CompilerParams(
+            collective_id=0, has_side_effects=True, vmem_limit_bytes=60 * 1024 * 1024
+        ),
+    )(matrix)
+
+
 def solution(mesh):
     in_specs = (P("row", "col"),)
     out_specs = (P("row", "col"), P(), P())
+    n_row, n_col = mesh.shape["row"], mesh.shape["col"]
+
+    def body(matrix):
+        square_plane = n_row == 2 * 2 * 2 and n_col == 2 * 2
+        if square_plane and matrix.shape[1] % TILE == 0 and matrix.shape[0] % 32 == 0:
+            return in_one_kernel(n_row, n_col, matrix)
+        return on_device(matrix)
+
     return jax.shard_map(
-        on_device, mesh=mesh, in_specs=in_specs, out_specs=out_specs, check_vma=False
+        body, mesh=mesh, in_specs=in_specs, out_specs=out_specs, check_vma=False
     )

time: 668 us -> 350 us (0.52)
  waiting for transfers between devices: 486 us -> 0 us
  Pallas kernels: 0 us -> 345 us
  blocking collectives: 90.8 us -> 0 us
  matrix products: 63.2 us -> 0 us
  between operations: 16.2 us -> 0.66 us
    all_gather x6 -> x0, waiting for transfers between devices: 485 us -> none  [the longest x2 188 us: on_device(): row_panel = lax.all_gather(rounded, 'col', axis=1, tiled=True)]
    pallas_call x0 -> x1, Pallas kernels: none -> 345 us  [in_one_kernel(): pl.pallas_call(functools.partial(kernel, n_row, n_col), out_shape=(jax.Sh...]
    psum x2 -> x0, blocking collectives: 90.8 us -> none  [the longest x1 51.2 us: on_device(): squares = lax.psum(jnp.sum(current * current), ('row', 'col'))]
    dot_general x4 -> x0, matrix products: 63.2 us -> none  [add_columns(): return jnp.dot(left_panel, portion, preferred_element_type=jnp.float32)]
  transfers between devices with their start and end apart: 6 -> 0, of which waited for: 6 -> 0; matrix products, arithmetic and copies ran while one was open for 0% -> 0% of each run, Pallas kernels for 0% -> 0%
where the time goes in v1:
time: 350 us
  Pallas kernels  345 us (99%)
  local copies, waits for them, and re-layouts  4.88 us (1%)
    pallas_call x1, Pallas kernels, in_one_kernel(): pl.pallas_call(functools.partial(kernel, n_row, n_col), out_shape=(jax.Sh...  345 us

profile of v1, /device:TPU:0, one launch (start us, length us, event | category | flops | bytes accessed | tf_op | source)
XLA Modules:
  0.0 350.3 jit_solution(2009900147368094302)
XLA Ops:
  0.6 344.8 %shard_map.38 = (f32[640,1280]{1,0:T(8,128)}, f32[2]{0:T(128)}, f32[2]{0:T(128)}) custom-call(f32[640,1280]{1,0:T(8,128)} %matrix_ref.1), custom_call_target="tpu_custom_call" | custom-call | tf_op jit(solution)/shard_map/pallas_call | solution.py:401
  345.4 0.0 copy-start.1
  345.4 0.0 copy-start
  345.4 3.8 %copy.7 = f32[640,1280]{1,0:T(8,128)} copy(f32[640,1280]{1,0:T(8,128)} %get-tuple-element.6) | data formatting | bytes 6553600
  349.3 0.0 copy-done.1
  349.3 0.5 copy.8
  349.8 0.0 copy-done
  349.8 0.5 copy.9
Async XLA Ops:
  345.4 3.9 %copy-start.1 = (f32[2]{0:T(128)S(1)}, f32[2]{0:T(128)}, u32[]{:S(2)}) copy-start(f32[2]{0:T(128)} %get-tuple-element.7) | copy-start | bytes 28
  345.4 4.4 %copy-start = (f32[2]{0:T(128)S(1)}, f32[2]{0:T(128)}, u32[]{:S(2)}) copy-start(f32[2]{0:T(128)} %get-tuple-element.8) | copy-start | bytes 28

commit v2 on v1

--- a/solution.py
+++ b/solution.py
@@ -59,6 +59,12 @@
 
 FROM_X, FROM_Y, FROM_SIB, SIB_X, SIB_Y, FROM_D, SIB_D = range(7)
 KINDS = 7
+LAG = 2
+
+
+def row_parts(rows):
+    fifth = rows // 5
+    return ((0, 2 * fifth), (2 * fifth, 2 * fifth), (4 * fifth, fifth))
 
 
 def kernel(
@@ -87,8 +93,10 @@
 ):
     rows, width = matrix_ref.shape
     tiles = width // TILE
-    half = rows // 2
     order = rows * n_row
+    panels = (panel1, panel2)
+    parts = row_parts(rows)
+    n_parts = len(parts)
     r = lax.axis_index("row")
     z = lax.axis_index("col")
     core = lax.rem(r, 2)
@@ -103,7 +111,6 @@
     relay_to = rx * (1 - core) + ry * core
     up = lax.rem(z + 1, n_col)
     down = lax.rem(z + n_col - 1, n_col)
-    opposite = lax.rem(z + 2, n_col)
 
     def load(t):
         return pltpu.make_async_copy(
@@ -131,87 +138,108 @@
         )
     pl.semaphore_wait(barrier, n_row + n_col - 2)
 
-    def rows_of(slot):
-        return pl.ds(pl.multiple_of(slot * rows, rows), rows)
+    def rows_of(slot, part=None):
+        offset, size = (0, rows) if part is None else parts[part]
+        return pl.ds(pl.multiple_of(slot * rows + offset, 16), size)
 
     def columns_of(slot, t):
         return pl.ds(pl.multiple_of(slot * width + t * TILE, TILE), TILE)
 
-    def xy(buf, phase, t, slot, kind, peer):
-        part = buf.at[t, rows_of(slot), :]
+    def xy(buf, step, part, t, slot, kind, peer):
+        block = buf.at[t, rows_of(slot, part), :]
+        phase = step * (n_parts + 1) + (0 if part is None else part + 1)
         return pltpu.make_async_remote_copy(
-            src_ref=part,
-            dst_ref=part,
+            src_ref=block,
+            dst_ref=block,
             send_sem=xy_send.at[phase, t, kind],
             recv_sem=xy_recv.at[phase, t, kind],
             device_id={"row": peer},
             device_id_type=MESH,
         )
 
-    def xy_start(buf, phase, t):
-        xy(buf, phase, t, r, FROM_X, rx).start()
-        xy(buf, phase, t, r, FROM_Y, ry).start()
-        xy(buf, phase, t, r, FROM_SIB, rs).start()
-
-    def xy_mid(buf, phase, t):
-        xy(buf, phase, t, rx, FROM_X, rx).wait_recv()
-        xy(buf, phase, t, ry, FROM_Y, ry).wait_recv()
-        xy(buf, phase, t, relay_from, FROM_D, relay_to).start()
-        xy(buf, phase, t, rx, SIB_X, rs).start()
-        xy(buf, phase, t, ry, SIB_Y, rs).start()
-
-    def xy_fin(buf, phase, t):
-        xy(buf, phase, t, rd, FROM_D, rd).wait_recv()
-        xy(buf, phase, t, rd, SIB_D, rs).start()
-
-    def xy_done(buf, phase, t):
-        xy(buf, phase, t, rs, FROM_SIB, rs).wait_recv()
-        xy(buf, phase, t, rx + to_sib, SIB_X, rs).wait_recv()
-        xy(buf, phase, t, ry + to_sib, SIB_Y, rs).wait_recv()
-        xy(buf, phase, t, rd + to_sib, SIB_D, rs).wait_recv()
-
-    def xy_sent(buf, phase, t):
-        xy(buf, phase, t, r, FROM_X, rx).wait_send()
-        xy(buf, phase, t, r, FROM_Y, ry).wait_send()
-        xy(buf, phase, t, r, FROM_SIB, rs).wait_send()
-        xy(buf, phase, t, rx, SIB_X, rs).wait_send()
-        xy(buf, phase, t, ry, SIB_Y, rs).wait_send()
-        xy(buf, phase, t, relay_from, FROM_D, relay_to).wait_send()
-        xy(buf, phase, t, rd, SIB_D, rs).wait_send()
-
-    def zc(panel, step, t, slot, kind, peer):
-        if kind < 2:
-            part = panel.at[:, columns_of(slot, t)]
-        else:
-            part = panel.at[pl.ds((kind - 2) * half, half), columns_of(slot, t)]
+    def xy_start(*to):
+        xy(*to, r, FROM_X, rx).start()
+        xy(*to, r, FROM_Y, ry).start()
+        xy(*to, r, FROM_SIB, rs).start()
+
+    def xy_mid(*to):
+        xy(*to, rx, FROM_X, rx).wait_recv()
+        xy(*to, ry, FROM_Y, ry).wait_recv()
+        xy(*to, relay_from, FROM_D, relay_to).start()
+        xy(*to, rx, SIB_X, rs).start()
+        xy(*to, ry, SIB_Y, rs).start()
+
+    def xy_fin(*to):
+        xy(*to, rd, FROM_D, rd).wait_recv()
+        xy(*to, rd, SIB_D, rs).start()
+
+    def xy_done(*to):
+        xy(*to, rs, FROM_SIB, rs).wait_recv()
+        xy(*to, rx + to_sib, SIB_X, rs).wait_recv()
+        xy(*to, ry + to_sib, SIB_Y, rs).wait_recv()
+        xy(*to, rd + to_sib, SIB_D, rs).wait_recv()
+
+    def xy_sent(*to):
+        xy(*to, r, FROM_X, rx).wait_send()
+        xy(*to, r, FROM_Y, ry).wait_send()
+        xy(*to, r, FROM_SIB, rs).wait_send()
+        xy(*to, rx, SIB_X, rs).wait_send()
+        xy(*to, ry, SIB_Y, rs).wait_send()
+        xy(*to, relay_from, FROM_D, relay_to).wait_send()
+        xy(*to, rd, SIB_D, rs).wait_send()
+
+    def zc(step, part, t, level, upward, slot, peer):
+        offset, size = parts[part]
+        block = panels[step].at[pl.ds(offset, size), columns_of(slot, t)]
+        kind = 2 * (level - 1) + upward
+        phase = step * n_parts + part
         return pltpu.make_async_remote_copy(
-            src_ref=part,
-            dst_ref=part,
-            send_sem=z_send.at[step, t, kind],
-            recv_sem=z_recv.at[step, t, kind],
+            src_ref=block,
+            dst_ref=block,
+            send_sem=z_send.at[phase, t, kind],
+            recv_sem=z_recv.at[phase, t, kind],
             device_id={"col": peer},
             device_id_type=MESH,
         )
 
-    def z_start(panel, step, t):
-        zc(panel, step, t, z, 0, up).start()
-        zc(panel, step, t, z, 1, down).start()
-
-    def z_mid(panel, step, t):
-        zc(panel, step, t, down, 0, up).wait_recv()
-        zc(panel, step, t, down, 2, up).start()
-        zc(panel, step, t, up, 1, down).wait_recv()
-        zc(panel, step, t, up, 3, down).start()
-
-    def z_fin(panel, step, t):
-        zc(panel, step, t, opposite, 2, up).wait_recv()
-        zc(panel, step, t, opposite, 3, down).wait_recv()
-
-    def z_sent(panel, step, t):
-        zc(panel, step, t, z, 0, up).wait_send()
-        zc(panel, step, t, z, 1, down).wait_send()
-        zc(panel, step, t, down, 2, up).wait_send()
-        zc(panel, step, t, up, 3, down).wait_send()
+    def z_send_level(step, part, t, level, act):
+        far = level - 1
+
+        @pl.when((z >= far) & (z < n_col - 1))
+        def _():
+            act(zc(step, part, t, level, 1, lax.rem(z + n_col - far, n_col), up))
+
+        @pl.when((z < n_col - far) & (z > 0))
+        def _():
+            act(zc(step, part, t, level, 0, lax.rem(z + far, n_col), down))
+
+    def z_wait_level(step, part, t, level):
+        @pl.when(z >= level)
+        def _():
+            zc(step, part, t, level, 1, lax.rem(z + n_col - level, n_col), up).wait_recv()
+
+        @pl.when(z < n_col - level)
+        def _():
+            zc(step, part, t, level, 0, lax.rem(z + level, n_col), down).wait_recv()
+
+    def z_start(step, part, t):
+        z_send_level(step, part, t, 1, lambda copy: copy.start())
+
+    def z_relay(step, part, t, level):
+        z_wait_level(step, part, t, level)
+        if level < n_col - 1:
+            z_send_level(step, part, t, level + 1, lambda copy: copy.start())
+
+    def z_sent(step, part, t):
+        for level in range(1, n_col):
+            z_send_level(step, part, t, level, lambda copy: copy.wait_send())
+
+    def over_tiles(work, start=0, stop=None):
+        def body(t, carry):
+            work(t)
+            return carry
+
+        lax.fori_loop(start, tiles if stop is None else stop, body, 0)
 
     def red_row(which, j, slot, peer):
         part = slots_row.at[which, slot]
@@ -283,88 +311,102 @@
         rounded = current[t].astype(jnp.bfloat16)
         panel1[:, columns_of(z, t)] = rounded
         cols[t, rows_of(r), :] = rounded
-        xy_start(cols, 0, t)
-        z_start(panel1, 0, t)
+        z_start(0, 0, t)
+        xy_start(cols, 0, None, t)
         wide = rounded.astype(jnp.float32)
         stats[4:5, :] += lanes(wide * wide)
     reduce_start(0, stats[...])
-    reduce_mid(0)
-
-    def product_phase(step, panel, scale):
-        phase = 2 * step
-
-        def mid(t, carry):
-            xy_mid(cols, phase, t)
-            z_mid(panel, step, t)
-            return carry
-
-        lax.fori_loop(0, tiles, mid, 0)
-
-        def fin(t, carry):
-            z_fin(panel, step, t)
-            return carry
-
-        lax.fori_loop(0, tiles, fin, 0)
-        xy_fin(cols, phase, 0)
-
-        def work(t, carry):
+
+    def step_of(step, scale_now, finish):
+        panel = panels[step]
+        last = n_parts - 1
+
+        def first_pass(t):
+            z_relay(step, 0, t, 1)
+            xy_mid(cols, step, None, t)
+
+        over_tiles(first_pass)
+        for level in range(2, n_col - 1):
+            over_tiles(lambda t: z_relay(step, 0, t, level))
+        over_tiles(lambda t: z_start(step, 1, t))
+        over_tiles(lambda t: xy_fin(cols, step, None, t))
+        over_tiles(lambda t: z_relay(step, 0, t, n_col - 1))
+        scale = scale_now()
+
+        for part in range(n_parts):
+            if part > 0:
+
+                def pass_one(t):
+                    z_relay(step, part, t, 1)
+                    xy_mid(squares, step, part - 1, t)
+
+                over_tiles(pass_one)
+                for level in range(2, n_col - 1):
+                    over_tiles(lambda t: z_relay(step, part, t, level))
+                if part < last:
+                    over_tiles(lambda t: z_start(step, part + 1, t))
+                over_tiles(lambda t: xy_fin(squares, step, part - 1, t))
+                over_tiles(lambda t: z_relay(step, part, t, n_col - 1))
+
+            def product_tile(t):
+                if part == 0:
+                    xy_done(cols, step, None, t)
+                offset, size = parts[part]
+                product = jnp.dot(
+                    panel[offset : offset + size, :],
+                    cols[t],
+                    preferred_element_type=jnp.float32,
+                )
+                if scale is not None:
+                    product = product * scale
+                squares[t, rows_of(r, part), :] = product.astype(jnp.bfloat16)
+                if part == 0:
+                    xy_sent(cols, step, None, t)
+                xy_start(squares, step, part, t)
+                if part == last:
+
+                    @pl.when(t >= LAG)
+                    def _():
+                        xy_mid(squares, step, part, t - LAG)
+
+            over_tiles(product_tile)
+
+        over_tiles(lambda t: xy_mid(squares, step, last, t), tiles - LAG)
+        xy_fin(squares, step, last, 0)
+
+        def cubic_tile(t):
             @pl.when(t < tiles - 1)
             def _():
-                xy_fin(cols, phase, t + 1)
-
-            xy_done(cols, phase, t)
-            product = jnp.dot(panel[...], cols[t], preferred_element_type=jnp.float32)
-            if scale is not None:
-                product = product * scale
-            squares[t, rows_of(r), :] = product.astype(jnp.bfloat16)
-            xy_sent(cols, phase, t)
-            xy_start(squares, phase + 1, t)
-            return carry
-
-        lax.fori_loop(0, tiles, work, 0)
-
-    def cubic_phase(step, panel, finish):
-        phase = 2 * step + 1
-
-        def mid(t, carry):
-            xy_mid(squares, phase, t)
-            return carry
-
-        lax.fori_loop(0, tiles, mid, 0)
-        xy_fin(squares, phase, 0)
-
-        def work(t, carry):
-            @pl.when(t < tiles - 1)
-            def _():
-                xy_fin(squares, phase, t + 1)
-
-            xy_done(squares, phase, t)
+                xy_fin(squares, step, last, t + 1)
+
+            for part in range(n_parts):
+                xy_done(squares, step, part, t)
             cubic = jnp.dot(panel[...], squares[t], preferred_element_type=jnp.float32)
-            xy_sent(squares, phase, t)
+            for part in range(n_parts):
+                xy_sent(squares, step, part, t)
             finish(t, cubic)
-            return carry
-
-        lax.fori_loop(0, tiles, work, 0)
-
-    total = reduce_end(0)
-    scale = target * order / (jnp.sum(total[4:5, :], axis=1, keepdims=True) + 1e-06)
-    root = jnp.sqrt(scale)
-
-    product_phase(0, panel1, scale)
+
+        over_tiles(cubic_tile)
+
+    roots = []
+
+    def first_scale():
+        reduce_mid(0)
+        total = reduce_end(0)
+        scale = target * order / (jnp.sum(total[4:5, :], axis=1, keepdims=True) + 1e-06)
+        roots.append(jnp.sqrt(scale))
+        return scale
 
     def finish_first(t, cubic):
         wide = panel1[:, columns_of(z, t)].astype(jnp.float32)
-        value = root * (1.5 * wide - 0.5 * cubic)
+        value = roots[0] * (1.5 * wide - 0.5 * cubic)
         current[t] = value
         rounded = value.astype(jnp.bfloat16)
         panel2[:, columns_of(z, t)] = rounded
         cols[t, rows_of(r), :] = rounded
-        xy_start(cols, 2, t)
-        z_start(panel2, 1, t)
+        z_start(1, 0, t)
+        xy_start(cols, 1, None, t)
         add_stats(0, t, value)
-
-    cubic_phase(0, panel1, finish_first)
-    product_phase(1, panel2, None)
 
     def finish_second(t, cubic):
         value = 1.5 * current[t] - 0.5 * cubic
@@ -372,7 +414,8 @@
         store(t).start()
         add_stats(2, t, value)
 
-    cubic_phase(1, panel2, finish_second)
+    step_of(0, first_scale, finish_first)
+    step_of(1, lambda: None, finish_second)
 
     reduce_start(1, stats[...])
     reduce_mid(1)
@@ -384,19 +427,20 @@
     frob_ref[0] = norms[1, 0]
     frob_ref[1] = norms[3, 0]
 
-    def clear(t, carry):
-        z_sent(panel1, 0, t)
-        z_sent(panel2, 1, t)
+    def clear(t):
+        for step in range(ITERS):
+            for part in range(n_parts):
+                z_sent(step, part, t)
         store(t).wait()
-        return carry
-
-    lax.fori_loop(0, tiles, clear, 0)
+
+    over_tiles(clear)
 
 
 def in_one_kernel(n_row, n_col, matrix):
     rows, width = matrix.shape
     tiles = width // TILE
     order = rows * n_row
+    n_parts = len(row_parts(rows))
     narrow = jnp.bfloat16
     return pl.pallas_call(
         functools.partial(kernel, n_row, n_col),
@@ -420,10 +464,10 @@
             pltpu.VMEM((8, 128), jnp.float32),
             pltpu.VMEM((2, n_row, 8, 128), jnp.float32),
             pltpu.VMEM((2, n_col, 8, 128), jnp.float32),
-            pltpu.SemaphoreType.DMA((2 * ITERS, tiles, KINDS)),
-            pltpu.SemaphoreType.DMA((2 * ITERS, tiles, KINDS)),
-            pltpu.SemaphoreType.DMA((ITERS, tiles, 4)),
-            pltpu.SemaphoreType.DMA((ITERS, tiles, 4)),
+            pltpu.SemaphoreType.DMA((ITERS * (n_parts + 1), tiles, KINDS)),
+            pltpu.SemaphoreType.DMA((ITERS * (n_parts + 1), tiles, KINDS)),
+            pltpu.SemaphoreType.DMA((ITERS * n_parts, tiles, 2 * (n_col - 1))),
+            pltpu.SemaphoreType.DMA((ITERS * n_parts, tiles, 2 * (n_col - 1))),
             pltpu.SemaphoreType.DMA((2, n_row + n_col)),
             pltpu.SemaphoreType.DMA((2, n_row + n_col)),
             pltpu.SemaphoreType.DMA((tiles,)),
@@ -442,7 +486,7 @@
 
     def body(matrix):
         square_plane = n_row == 2 * 2 * 2 and n_col == 2 * 2
-        if square_plane and matrix.shape[1] % TILE == 0 and matrix.shape[0] % 32 == 0:
+        if square_plane and matrix.shape[1] % TILE == 0 and matrix.shape[0] % (5 * 16) == 0:
             return in_one_kernel(n_row, n_col, matrix)
         return on_device(matrix)
 

time: 350 us -> 293 us (0.84)
  Pallas kernels: 345 us -> 288 us
    pallas_call x1, Pallas kernels: 345 us -> 288 us  [in_one_kernel(): pl.pallas_call(functools.partial(kernel, n_row, n_col), out_shape=(jax.Sh...]
where the time goes in v2:
time: 293 us
  Pallas kernels  288 us (98%)
  local copies, waits for them, and re-layouts  4.88 us (2%)
    pallas_call x1, Pallas kernels, in_one_kernel(): pl.pallas_call(functools.partial(kernel, n_row, n_col), out_shape=(jax.Sh...  288 us

profile of v2, /device:TPU:0, one launch (start us, length us, event | category | flops | bytes accessed | tf_op | source)
XLA Modules:
  0.0 293.3 jit_solution(6082714770252857281)
XLA Ops:
  0.6 287.8 %shard_map.38 = (f32[640,1280]{1,0:T(8,128)}, f32[2]{0:T(128)}, f32[2]{0:T(128)}) custom-call(f32[640,1280]{1,0:T(8,128)} %matrix_ref.1), custom_call_target="tpu_custom_call" | custom-call | tf_op jit(solution)/shard_map/pallas_call | solution.py:445
  288.4 0.0 copy-start.1
  288.4 0.0 copy-start
  288.4 3.8 %copy.7 = f32[640,1280]{1,0:T(8,128)} copy(f32[640,1280]{1,0:T(8,128)} %get-tuple-element.6) | data formatting | bytes 6553600
  292.3 0.0 copy-done.1
  292.3 0.5 copy.8
  292.8 0.0 copy-done
  292.8 0.5 copy.9
Async XLA Ops:
  288.4 3.9 %copy-start.1 = (f32[2]{0:T(128)S(1)}, f32[2]{0:T(128)}, u32[]{:S(2)}) copy-start(f32[2]{0:T(128)} %get-tuple-element.7) | copy-start | bytes 28
  288.4 4.4 %copy-start = (f32[2]{0:T(128)S(1)}, f32[2]{0:T(128)}, u32[]{:S(2)}) copy-start(f32[2]{0:T(128)} %get-tuple-element.8) | copy-start | bytes 28

commit v3 on v2

--- a/solution.py
+++ b/solution.py
@@ -89,7 +89,6 @@
     red_send,
     red_recv,
     load_sem,
-    store_sem,
 ):
     rows, width = matrix_ref.shape
     tiles = width // TILE
@@ -117,13 +116,6 @@
             matrix_ref.at[:, pl.ds(t * TILE, TILE)], current.at[t], load_sem.at[t]
         )
 
-    def store(t):
-        return pltpu.make_async_copy(
-            current.at[t],
-            out_ref.at[:, pl.ds(pl.multiple_of(t * TILE, TILE), TILE)],
-            store_sem.at[t],
-        )
-
     for t in range(tiles):
         load(t).start()
 
@@ -410,8 +402,7 @@
 
     def finish_second(t, cubic):
         value = 1.5 * current[t] - 0.5 * cubic
-        current[t] = value
-        store(t).start()
+        out_ref[:, pl.ds(pl.multiple_of(t * TILE, TILE), TILE)] = value
         add_stats(2, t, value)
 
     step_of(0, first_scale, finish_first)
@@ -431,7 +422,6 @@
         for step in range(ITERS):
             for part in range(n_parts):
                 z_sent(step, part, t)
-        store(t).wait()
 
     over_tiles(clear)
 
@@ -445,13 +435,13 @@
     return pl.pallas_call(
         functools.partial(kernel, n_row, n_col),
         out_shape=(
-            jax.ShapeDtypeStruct((rows, width), jnp.float32),
+            pltpu.VMEM((rows, width), jnp.float32),
             jax.ShapeDtypeStruct((ITERS,), jnp.float32),
             jax.ShapeDtypeStruct((ITERS,), jnp.float32),
         ),
         in_specs=[pl.BlockSpec(memory_space=pl.ANY)],
         out_specs=(
-            pl.BlockSpec(memory_space=pl.ANY),
+            pl.BlockSpec(memory_space=pltpu.VMEM),
             pl.BlockSpec(memory_space=pltpu.SMEM),
             pl.BlockSpec(memory_space=pltpu.SMEM),
         ),
@@ -471,10 +461,9 @@
             pltpu.SemaphoreType.DMA((2, n_row + n_col)),
             pltpu.SemaphoreType.DMA((2, n_row + n_col)),
             pltpu.SemaphoreType.DMA((tiles,)),
-            pltpu.SemaphoreType.DMA((tiles,)),
         ],
         compiler_params=pltpu.CompilerParams(
-            collective_id=0, has_side_effects=True, vmem_limit_bytes=60 * 1024 * 1024
+            collective_id=0, has_side_effects=True, vmem_limit_bytes=56 * 1024 * 1024
         ),
     )(matrix)
 

time: 293 us -> 291 us (level)
  no operation moved by 1% of the time
where the time goes in v3:
time: 291 us
  Pallas kernels  288 us (99%)
    pallas_call x1, Pallas kernels, in_one_kernel(): pl.pallas_call(functools.partial(kernel, n_row, n_col), out_shape=(pltpu....  288 us

profile of v3, /device:TPU:0, one launch (start us, length us, event | category | flops | bytes accessed | tf_op | source)
XLA Modules:
  0.0 291.1 jit_solution(7679117422085795566)
XLA Ops:
  0.6 287.7 %shard_map.38 = (f32[640,1280]{1,0:T(8,128)S(1)}, f32[2]{0:T(128)}, f32[2]{0:T(128)}) custom-call(f32[640,1280]{1,0:T(8,128)} %matrix_ref.1), custom_call_target="tpu_custom_call" | custom-call | tf_op jit(solution)/shard_map/pallas_call | solution.py:435
  288.4 0.0 copy-start.1
  288.4 0.0 copy-start
  288.4 1.7 copy.7
  290.1 0.0 copy-done.1
  290.1 0.5 copy.8
  290.6 0.0 copy-done
  290.6 0.5 copy.9
Async XLA Ops:
  288.4 1.7 copy-start.1
  288.4 2.2 copy-start
